TPU v7x, 32 devices: a whole 2x2x4 slice. The times are simulated.
32 devices in a mesh: freq: 2 (over y), rcv: 4 (over z), src: 4 (over x, core).
Axes of the slice: x: 2, y: 2, z: 4, core: 2. Of those that a mesh axis runs over, the one named last changes fastest.
Arguments:
- traces: float32 [256, 2, 4096], P(('freq', 'src'), None, 'rcv'), parts along dimension 0, may hold values from -6 to 6
- moveout: float32 [2, 64, 16], P(None, 'freq'), parts along dimension 1, may hold values from -0.75 to 0.75
- trace_owner: int32 [8192], P(('freq', 'rcv')), parts along dimension 0, may hold values from 0 to 3, as said below
- trace_group: int32 [8192], P(('freq', 'rcv')), parts along dimension 0, may hold values from 0 to 127
- trace_table: int32 [8192], P(('freq', 'rcv')), parts along dimension 0, may hold values from 0 to 31
- aperture: float32 [2, 16384, 8192], P(None, ('freq', 'rcv'), 'src'), parts along dimension 1, may hold values from -0.046875 to 0.046875
- shaping: float32 [256, 2, 8192], P(('freq', 'src'), None, 'rcv'), parts along dimension 0, may hold values from -0.5 to 0.5
Outputs:
- demultiple: float32 [256, 2, 8192], P(('freq', 'src'), None, 'rcv'), parts along dimension 0
There are 2 independent parts, one for each index of `freq`. A program takes and returns all parts, laid end to end along the dimension named above; each array names one. Nothing has to cross between parts.
Inputs may be any that keep to these rules, and one draw needn't show every extreme that they name: `trace_owner`: among the 1024 traces of each index of rcv (aligned blocks of the array), at most 512 name the same owner, and in every draw some owner is named by exactly 512 traces of every block.
All inputs are finite; a program needn't handle non-finite values.
Results may differ from a plain program's by a relative error of at most 0.0001.
Values sent between devices are 32-bit elements; how exact they have to be, the bound alone decides.
A program may use at most 128 MiB of HBM per device.

v0:
```python
import jax
import jax.numpy as jnp
from jax import lax
from jax.sharding import PartitionSpec as P

ITERS = 2


def from_root(value, axis, source):
    kept = jnp.where(lax.axis_index(axis) == source, value, 0).astype(value.dtype)
    return lax.psum(kept, axis)


def complex_join(partial_terms):
    return jnp.stack(
        [
            partial_terms[:, 0, 0] - partial_terms[:, 1, 1],
            partial_terms[:, 0, 1] + partial_terms[:, 1, 0],
        ],
        axis=1,
    )


def complex_product(left_side, right_side):
    real_part = left_side[:, 0] * right_side[:, 0] - left_side[:, 1] * right_side[:, 1]
    imag_part = left_side[:, 0] * right_side[:, 1] + left_side[:, 1] * right_side[:, 0]
    return jnp.stack([real_part, imag_part], axis=1)


def bin_matrix(group_code, table_code, moveout, groups, owner_mask):
    group_hot = (group_code[:, None] == jnp.arange(groups)[None, :]).astype(jnp.float32)
    group_hot = group_hot * owner_mask[:, None]
    table_hot = (table_code[:, None] == jnp.arange(moveout.shape[1])[None, :]).astype(jnp.float32)
    weights = jnp.einsum("tk,ckj->tcj", table_hot, moveout, precision=lax.Precision.HIGHEST)
    matrix = group_hot[:, None, :, None] * weights[:, :, None, :]
    return matrix.reshape(matrix.shape[0], 2, groups * moveout.shape[2])


def interpolate(values, matrix):
    return complex_join(
        jnp.einsum("sct,tdb->scdb", values, matrix, precision=lax.Precision.HIGHEST)
    )


def to_columns(panel_now):
    shots_all = lax.all_gather(panel_now, "src", axis=0, tiled=True)
    fold_count = lax.axis_size("rcv") // lax.axis_size("src")
    first_root = fold_count * lax.axis_index("src")
    pieces = [from_root(shots_all, "rcv", first_root + offset) for offset in range(fold_count)]
    return jnp.concatenate(pieces, axis=2)


def multiply(columns, aperture):
    return lax.psum_scatter(
        complex_join(
            jnp.einsum("sck,dik->scdi", columns, aperture, precision=lax.Precision.HIGHEST)
        ),
        "src",
        scatter_dimension=0,
        tiled=True,
    )


def per_device(traces, moveout, trace_owner, trace_group, trace_table, aperture, shaping):
    groups = aperture.shape[1] // moveout.shape[2]

    def one_owner(owner_index):
        owner_mask = (trace_owner == owner_index).astype(jnp.float32)
        matrix = bin_matrix(trace_group, trace_table, moveout, groups, owner_mask)
        return interpolate(traces, matrix)

    binned = lax.psum_scatter(
        lax.map(one_owner, jnp.arange(1 * lax.axis_size("rcv"), dtype=jnp.int32)),
        "rcv",
        scatter_dimension=0,
        tiled=True,
    )[0]
    panel_now = binned
    for sweep_index in range(ITERS):
        multiples = multiply(to_columns(panel_now), aperture)
        panel_now = binned - complex_product(shaping, multiples)
    return panel_now


def solution(mesh):
    in_specs = (
        P(("freq", "src"), None, "rcv"),
        P(None, "freq", None),
        P(("freq", "rcv")),
        P(("freq", "rcv")),
        P(("freq", "rcv")),
        P(None, ("freq", "rcv"), "src"),
        P(("freq", "src"), None, "rcv"),
    )
    out_specs = P(("freq", "src"), None, "rcv")
    return jax.shard_map(
        per_device, mesh=mesh, in_specs=in_specs, out_specs=out_specs, check_vma=False
    )
```

profile of v0, /device:TPU:0, one launch (start us, length us, event | category | flops | bytes accessed | tf_op | source)
XLA Modules:
  0.0 581.3 jit_solution(2520688945853668558)
XLA Ops:
  7.6 160.8 %while.10 = (s32[]{:T(128)}, f32[4,32,2,2048]{3,1,2,0:T(8,128)}, s32[1024]{0:T(1024)}, s32[4]{0:T(128)S(1)}, s32[1024]{0:T(1024)}, /*index=5*/s32[1024]{0:T(1024...) while((s32[]{:T(128)}, f32[4,32,2,2048]{3,1,2,0:T(8,128)}, s32[1024]{0:T(1024)}, s32[4]{0:T(128)S(1)}, ...), condition=%wide.region_1.2_spmd, body=%wide.region_0.1_spmd.sunk | while | flops 3238561792 | bytes 55632548 | solution.py:73
  8.2 1.3 compare_convert_fusion.2
  10.3 4.3 mul.92
  14.8 12.2 %bitcast_multiply_fusion.2 = f32[1024,2,2048]{0,2,1:T(8,128)} fusion(f32[1024,2,16]{0,2,1:T(8,128)S(1)} %bitcast.96, f32[1024,2048]{0,1:T(8,128)} %bitcast.95), kind=kLoop, calls=%fused_computation.2.clone.1 | loop fusion | flops 4194304 | bytes 25296896 | tf_op jit(solution)/shard_map/while/body/eval_jaxpr/mul | solution.py:35
  27.1 19.8 %fusion.39 = f32[32,2,2,2048]{3,0,1,2:T(8,128)S(1)} fusion(f32[1024,2,2048]{0,2,1:T(8,128)} %bitcast_multiply_fusion.2, f32[32,2,1024]{2,0,1:T(8,128)S(1)} %get-tuple-element.164), kind=kOutput, calls=%fused_computation.3.clone.1 | convolution fusion | flops 3221225472 | bytes 18087936 | tf_op jit(solution)/shard_map/while/body/eval_jaxpr/sct,tdb->scdb/dot_general | solution.py:41
  48.4 1.3 compare_convert_fusion.2
  50.5 4.3 mul.92
  55.0 12.2 %bitcast_multiply_fusion.2 = f32[1024,2,2048]{0,2,1:T(8,128)} fusion(f32[1024,2,16]{0,2,1:T(8,128)S(1)} %bitcast.96, f32[1024,2048]{0,1:T(8,128)} %bitcast.95), kind=kLoop, calls=%fused_computation.2.clone.1 | loop fusion | flops 4194304 | bytes 25296896 | tf_op jit(solution)/shard_map/while/body/eval_jaxpr/mul | solution.py:35
  67.3 19.8 %fusion.39 = f32[32,2,2,2048]{3,0,1,2:T(8,128)S(1)} fusion(f32[1024,2,2048]{0,2,1:T(8,128)} %bitcast_multiply_fusion.2, f32[32,2,1024]{2,0,1:T(8,128)S(1)} %get-tuple-element.164), kind=kOutput, calls=%fused_computation.3.clone.1 | convolution fusion | flops 3221225472 | bytes 18087936 | tf_op jit(solution)/shard_map/while/body/eval_jaxpr/sct,tdb->scdb/dot_general | solution.py:41
  88.6 1.3 compare_convert_fusion.2
  90.7 4.3 mul.92
  95.2 12.2 %bitcast_multiply_fusion.2 = f32[1024,2,2048]{0,2,1:T(8,128)} fusion(f32[1024,2,16]{0,2,1:T(8,128)S(1)} %bitcast.96, f32[1024,2048]{0,1:T(8,128)} %bitcast.95), kind=kLoop, calls=%fused_computation.2.clone.1 | loop fusion | flops 4194304 | bytes 25296896 | tf_op jit(solution)/shard_map/while/body/eval_jaxpr/mul | solution.py:35
  107.5 19.8 %fusion.39 = f32[32,2,2,2048]{3,0,1,2:T(8,128)S(1)} fusion(f32[1024,2,2048]{0,2,1:T(8,128)} %bitcast_multiply_fusion.2, f32[32,2,1024]{2,0,1:T(8,128)S(1)} %get-tuple-element.164), kind=kOutput, calls=%fused_computation.3.clone.1 | convolution fusion | flops 3221225472 | bytes 18087936 | tf_op jit(solution)/shard_map/while/body/eval_jaxpr/sct,tdb->scdb/dot_general | solution.py:41
  128.8 1.3 compare_convert_fusion.2
  130.9 4.3 mul.92
  135.4 12.2 %bitcast_multiply_fusion.2 = f32[1024,2,2048]{0,2,1:T(8,128)} fusion(f32[1024,2,16]{0,2,1:T(8,128)S(1)} %bitcast.96, f32[1024,2048]{0,1:T(8,128)} %bitcast.95), kind=kLoop, calls=%fused_computation.2.clone.1 | loop fusion | flops 4194304 | bytes 25296896 | tf_op jit(solution)/shard_map/while/body/eval_jaxpr/mul | solution.py:35
  147.6 19.8 %fusion.39 = f32[32,2,2,2048]{3,0,1,2:T(8,128)S(1)} fusion(f32[1024,2,2048]{0,2,1:T(8,128)} %bitcast_multiply_fusion.2, f32[32,2,1024]{2,0,1:T(8,128)S(1)} %get-tuple-element.164), kind=kOutput, calls=%fused_computation.3.clone.1 | convolution fusion | flops 3221225472 | bytes 18087936 | tf_op jit(solution)/shard_map/while/body/eval_jaxpr/sct,tdb->scdb/dot_general | solution.py:41
  168.5 46.5 %reduce-scatter.4.cloned.1.call-done = f32[1,32,2,2048]{3,1,2,0:T(8,128)} async-done(((f32[4,32,2,2048]{3,1,2,0:T(8,128)}), f32[1,32,2,2048]{3,1,2,0:T(8,128)}) %reduce-scatter.4.cloned.1.call-update) | async-done | bytes 524304 | tf_op jit(solution)/shard_map/reduce_scatter | solution.py:72
  215.0 23.3 %all-gather.6.cloned.1.call-done = f32[1,128,2,2048]{3,1,2,0:T(8,128)} async-done(((f32[1,32,2,2048]{3,1,2,0:T(8,128)}), f32[1,128,2,2048]{3,1,2,0:T(8,128)}) %all-gather.6.cloned.1.call-update) | async-done | bytes 2097168 | tf_op jit(solution)/shard_map/all_gather | solution.py:46
  238.3 3.1 select_bitcast_fusion
  241.7 85.9 %all-reduce.3.cloned.1.call-done = f32[128,2,2048]{2,0,1:T(8,128)} async-done(((f32[128,2,2048]{2,0,1:T(8,128)}), f32[128,2,2048]{2,0,1:T(8,128)}) %all-reduce.3.cloned.1.call-update) | async-done | bytes 2097168 | tf_op jit(solution)/shard_map/psum | solution.py:11
  327.6 33.0 %fusion.15 = f32[128,2,2,2048]{3,0,2,1:T(8,128)S(1)} fusion(f32[2,2048,2048]{2,1,0:T(8,128)} %param.14, f32[128,2,2048]{2,0,1:T(8,128)} %all-reduce.3.cloned.1.call-done), kind=kOutput, calls=%fused_computation.21 | convolution fusion | flops 25769803776 | bytes 39845888 | tf_op jit(solution)/shard_map/sck,dik->scdi/dot_general | solution.py:56
  360.9 1.5 pad_maximum_fusion
  363.8 28.9 %reduce-scatter.6.cloned.1.call-done = f32[32,2,2048]{2,0,1:T(8,128)} async-done(((f32[128,2,2048]{2,0,1:T(8,128)}), f32[32,2,2048]{2,0,1:T(8,128)}) %reduce-scatter.6.cloned.1.call-update) | async-done | bytes 524304 | tf_op jit(solution)/shard_map/reduce_scatter | solution.py:54
  392.7 1.2 multiply_subtract_fusion.1
  394.9 22.7 %all-gather.4.cloned.1.call-done = f32[128,2,2048]{2,0,1:T(8,128)} async-done(((f32[32,2,2048]{2,0,1:T(8,128)}), f32[128,2,2048]{2,0,1:T(8,128)}) %all-gather.4.cloned.1.call-update) | async-done | bytes 2097168 | tf_op jit(solution)/shard_map/all_gather | solution.py:46
  417.6 3.1 broadcast_select_fusion
  421.0 85.9 %all-reduce.5.cloned.1.call-done = f32[128,2,2048]{2,0,1:T(8,128)} async-done(((f32[128,2,2048]{2,0,1:T(8,128)}), f32[128,2,2048]{2,0,1:T(8,128)}) %all-reduce.5.cloned.1.call-update) | async-done | bytes 2097168 | tf_op jit(solution)/shard_map/psum | solution.py:11
  506.9 33.0 %fusion.13 = f32[128,2,2,2048]{3,0,2,1:T(8,128)S(1)} fusion(f32[2,2048,2048]{2,1,0:T(8,128)} %param.14, f32[128,2,2048]{2,0,1:T(8,128)} %all-reduce.5.cloned.1.call-done), kind=kOutput, calls=%fused_computation.19 | convolution fusion | flops 25769803776 | bytes 39845888 | tf_op jit(solution)/shard_map/sck,dik->scdi/dot_general | solution.py:56
  540.1 1.5 pad_maximum_fusion.1
  541.6 30.3 %reduce-scatter.8.cloned.1.call-done = f32[32,2,2048]{2,0,1:T(8,128)} async-done(((f32[128,2,2048]{2,0,1:T(8,128)}), f32[32,2,2048]{2,0,1:T(8,128)}) %reduce-scatter.8.cloned.1.call-update) | async-done | bytes 524304 | tf_op jit(solution)/shard_map/reduce_scatter | solution.py:54
  572.0 1.2 multiply_subtract_fusion
  (67 shorter events, 15.7 us)
Async XLA Ops:
  6.5 208.4 %reduce-scatter.4.cloned.1.call-start = ((), (), s32[]{:S(2)}) async-start(), calls=%async_computation.3 | async-start | bytes 2621440 | tf_op jit(solution)/shard_map/reduce_scatter | solution.py:72
  10.3 4.4 copy-start.2
  10.3 4.3 copy-start.3
  50.5 4.4 copy-start.2
  50.5 4.3 copy-start.3
  90.7 4.4 copy-start.2
  90.7 4.3 copy-start.3
  130.9 4.4 copy-start.2
  130.9 4.3 copy-start.3
  168.4 69.9 %all-gather.6.cloned.1.call-start = ((), (), s32[]{:S(2)}) async-start(), calls=%async_computation.9 | async-start | bytes 2621440 | tf_op jit(solution)/shard_map/all_gather | solution.py:46
  214.9 112.7 %all-reduce.3.cloned.1.call-start = ((), (), s32[]{:S(2)}) async-start(), calls=%async_computation.4 | async-start | bytes 4194304 | tf_op jit(solution)/shard_map/psum | solution.py:11
  241.4 151.2 %reduce-scatter.6.cloned.1.call-start = ((), (), s32[]{:S(2)}) async-start(), calls=%async_computation.5 | async-start | bytes 2621440 | tf_op jit(solution)/shard_map/reduce_scatter | solution.py:54
  362.3 1.0 copy-start.1
  362.3 31.6 %copy-start = (f32[1,32,2,2048]{3,1,2,0:T(8,128)S(1)}, f32[1,32,2,2048]{3,1,2,0:T(8,128)}, u32[]{:S(2)}) copy-start(f32[1,32,2,2048]{3,1,2,0:T(8,128)} %reduce-scatter.4.cloned.1.call-done) | copy-start | bytes 1572868
  362.4 55.2 %all-gather.4.cloned.1.call-start = ((), (), s32[]{:S(2)}) async-start(), calls=%async_computation.6 | async-start | bytes 2621440 | tf_op jit(solution)/shard_map/all_gather | solution.py:46
  394.8 112.1 %all-reduce.5.cloned.1.call-start = ((), (), s32[]{:S(2)}) async-start(), calls=%async_computation.7 | async-start | bytes 4194304 | tf_op jit(solution)/shard_map/psum | solution.py:11
  420.7 151.2 %reduce-scatter.8.cloned.1.call-start = ((), (), s32[]{:S(2)}) async-start(), calls=%async_computation.8 | async-start | bytes 2621440 | tf_op jit(solution)/shard_map/reduce_scatter | solution.py:54
Sparse Core Ops, SparseCore 0:
  168.5 46.3 reduce-scatter.3
  216.5 21.7 all-gather.5
  241.6 86.0 all-reduce.2
  362.5 30.1 reduce-scatter.5
  394.9 22.5 all-gather.3
  420.8 86.0 all-reduce.4
  541.8 30.1 reduce-scatter.7
where the time goes:
time: 582 us; the launch traced here: 581 us
  waiting for transfers between devices  324 us (56%)
  matrix products  146 us (25%)
  other arithmetic  73.9 us (13%)
  local copies, waits for them, and re-layouts  23.4 us (4%)
  between operations  13.6 us (2%)
    psum x2, waiting for transfers between devices, from_root(): return lax.psum(kept, axis)  172 us
    dot_general x4, matrix products, interpolate(): jnp.einsum('sct,tdb->scdb', values, matrix, precision=lax.Precision.HIGHEST)  79.2 us
    dot_general x2, matrix products, multiply(): jnp.einsum('sck,dik->scdi', columns, aperture, precision=lax.Precision.HI...  66 us
    reduce_scatter x2, waiting for transfers between devices, multiply(): lax.psum_scatter(complex_join(jnp.einsum('sck,dik->scdi', columns, apertu...  59.2 us
    mul x4, other arithmetic, bin_matrix(): matrix = group_hot[:, None, :, None] * weights[:, :, None, :]  48.9 us
    reduce_scatter x1, waiting for transfers between devices, per_device(): lax.psum_scatter(lax.map(one_owner, jnp.arange(1 * lax.axis_size('rcv'),...  46.5 us
    all_gather x2, waiting for transfers between devices, to_columns(): shots_all = lax.all_gather(panel_now, 'src', axis=0, tiled=True)  46 us
    mul x4, local copies, waits for them, and re-layouts, bin_matrix(): matrix = group_hot[:, None, :, None] * weights[:, :, None, :]  17.3 us
  transfers between devices with their start and end apart: 7, of which 7 were waited for; matrix products, arithmetic and copies ran while one was open for 0% of the time, Pallas kernels for 0%

commit v1 on v0

v1 whole, which is shorter than its diff:
```python
import functools

import jax
import jax.numpy as jnp
from jax import lax
from jax.experimental import pallas as pl
from jax.experimental.pallas import tpu as pltpu
from jax.sharding import PartitionSpec as P

ITERS = 2
MESH = pl.DeviceIdType.MESH
F32 = jnp.float32
BF16 = jnp.bfloat16
NT = (((1,), (1,)), ((), ()))


def split(value):
    high = value.astype(BF16)
    return high, (value - high.astype(F32)).astype(BF16)


def remote(src, dst, send_sem, recv_sem, where):
    return pltpu.make_async_remote_copy(
        src_ref=src,
        dst_ref=dst,
        send_sem=send_sem,
        recv_sem=recv_sem,
        device_id=where,
        device_id_type=MESH,
    )


def pieces(refs_shape, count):
    planes, rows = refs_shape[0], refs_shape[1]
    per = max(1, count // planes)
    step = rows // per
    return [(p, pl.ds(h * step, step)) for p in range(planes) for h in range(per)]


def gather_kernel(nz, ns, fold, plane, cuts, in_ref, out_ref, *scratch):
    if plane:
        held, zs, zr, ps, pr, ls = scratch
    else:
        held = out_ref
        zs, zr, ls = scratch
    z = lax.axis_index("rcv")
    c = lax.axis_index("src")
    width = in_ref.shape[-1]
    rows = in_ref.shape[1]

    barrier = pltpu.get_barrier_semaphore()
    for way in (1, -1):
        near = z + way

        @pl.when((near >= 0) & (near < nz))
        def _():
            pl.semaphore_signal(barrier, inc=1, device_id={"rcv": near}, device_id_type=MESH)

    if plane:
        for off in range(1, ns):
            pl.semaphore_signal(
                barrier, inc=1, device_id={"src": lax.rem(c + off, ns)}, device_id_type=MESH
            )
    peers = jnp.where(z > 0, 1, 0) + jnp.where(z < nz - 1, 1, 0)
    pl.semaphore_wait(barrier, peers + (ns - 1 if plane else 0))

    def along(src, block, lane, dist, q):
        way = 1 - 2 * lane
        cut = cuts[q]
        return remote(
            src.at[cut] if src is in_ref else src.at[(block,) + cut],
            held.at[(block,) + cut],
            zs.at[lane, dist, q],
            zr.at[lane, dist, q],
            {"rcv": z + way},
        )

    def place(who, f, q):
        p, r = cuts[q]
        return out_ref.at[
            p, pl.ds(pl.multiple_of(who * rows + r.start, 8), r.size), pl.ds(f * width, width)
        ]

    def across(src, block, q):
        f = block - (block // fold) * fold
        cut = cuts[q]
        return remote(
            src.at[cut] if src is in_ref else src.at[(block,) + cut],
            place(c, f, q),
            ps.at[block, q],
            pr.at[c, f, q],
            {"src": block // fold},
        )

    def local(src, block, q):
        f = block - (block // fold) * fold if plane else 0
        cut = cuts[q]
        there = place(c, f, q) if plane else held.at[(block,) + cut]
        here = src.at[cut] if src is in_ref else src.at[(block,) + cut]
        return pltpu.make_async_copy(here, there, ls.at[f, q])

    def hand_on(src, block, q):
        if not plane:
            return

        @pl.when(block // fold != c)
        def _():
            across(src, block, q).start()

        @pl.when(block // fold == c)
        def _():
            local(src, block, q).start()

    def has(lane):
        near = z + 1 - 2 * lane
        return (near >= 0) & (near < nz)

    for q in range(len(cuts)):
        for lane in (0, 1):

            @pl.when(has(lane))
            def _():
                along(in_ref, z, lane, 0, q).start()

        if plane:
            hand_on(in_ref, z, q)
        else:
            local(in_ref, z, q).start()

    def hop(dist, carry):
        for q in range(len(cuts)):
            for lane in (0, 1):
                block = z - dist * (1 - 2 * lane)

                @pl.when((block >= 0) & (block < nz))
                def _():
                    along(held, block, lane, dist - 1, q).wait_recv()

                    @pl.when(has(lane))
                    def _():
                        along(held, block, lane, dist, q).start()

                    hand_on(held, block, q)

        return carry

    lax.fori_loop(1, nz, hop, 0)

    def drain(dist, carry):
        for q in range(len(cuts)):
            for lane in (0, 1):
                block = z - dist * (1 - 2 * lane)

                @pl.when((block >= 0) & (block < nz) & has(lane))
                def _():
                    along(held, block, lane, dist, q).wait_send()

            if plane:

                @pl.when(dist // fold != c)
                def _():
                    across(held, dist, q).wait_send()

                @pl.when(dist // fold == c)
                def _():
                    local(held, dist, q).wait()

        return carry

    lax.fori_loop(0, nz, drain, 0)
    for q in range(len(cuts)):
        if not plane:
            local(in_ref, z, q).wait()
        else:
            for off in range(1, ns):
                who = lax.rem(c + off, ns)
                for f in range(fold):
                    remote(
                        place(who, f, q),
                        place(who, f, q),
                        ps.at[0, q],
                        pr.at[who, f, q],
                        {"src": who},
                    ).wait_recv()


def gather(value, nz, ns, plane, count, cid, name):
    planes, rows, width = value.shape
    fold = nz // ns
    cuts = pieces(value.shape, count)
    nq = len(cuts)
    dma = pltpu.SemaphoreType.DMA
    scratch = [dma((2, nz, nq)), dma((2, nz, nq))]
    if plane:
        out = jax.ShapeDtypeStruct((planes, ns * rows, fold * width), F32)
        scratch = [pltpu.VMEM((nz,) + value.shape, F32)] + scratch
        scratch += [dma((nz, nq)), dma((ns, fold, nq)), dma((fold, nq))]
    else:
        out = jax.ShapeDtypeStruct((nz,) + value.shape, F32)
        scratch += [dma((1, nq))]
    return pl.pallas_call(
        functools.partial(gather_kernel, nz, ns, fold, plane, cuts),
        out_shape=out,
        in_specs=[pl.BlockSpec(memory_space=pltpu.VMEM)],
        out_specs=pl.BlockSpec(memory_space=pltpu.VMEM),
        scratch_shapes=scratch,
        name=name,
        compiler_params=pltpu.CompilerParams(collective_id=cid, has_side_effects=True),
    )(value)


def bin_kernel(groups, tables, shots, wt_ref, x_ref, out_ref):
    stencil = wt_ref.shape[0] // 2
    rows = 2 * shots
    width = x_ref.shape[-1]
    me = lax.axis_index("rcv").astype(F32)
    owner = x_ref[0, 0, rows : rows + 1, :]
    group = x_ref[0, 0, rows + 1 : rows + 2, :]
    table = x_ref[0, 0, rows + 2 : rows + 3, :]
    table_ids = lax.broadcasted_iota(jnp.int32, (tables, width), 0).astype(F32)
    table_hot = (table_ids == table).astype(BF16)
    w = wt_ref[...]
    w0 = w.astype(BF16)
    rest = w - w0.astype(F32)
    w1 = rest.astype(BF16)
    w2 = (rest - w1.astype(F32)).astype(BF16)
    picked = sum(
        jnp.dot(part, table_hot, preferred_element_type=F32) for part in (w0, w1, w2)
    )
    group_ids = lax.broadcasted_iota(jnp.int32, (groups, width), 0).astype(F32)
    hot = ((group_ids == group) & (owner == me)).astype(BF16)
    real = x_ref[0, 0, 0:shots, :]
    imag = x_ref[0, 0, shots:rows, :]

    @pl.when(pl.program_id(0) == 0)
    def _():
        out_ref[...] = jnp.zeros_like(out_ref)

    for j in range(stencil):
        wr = picked[j : j + 1, :]
        wi = picked[stencil + j : stencil + j + 1, :]
        both = jnp.concatenate([real * wr - imag * wi, real * wi + imag * wr], axis=0)
        high, low = split(both)
        total = lax.dot_general(high, hot, NT, preferred_element_type=F32)
        total += lax.dot_general(low, hot, NT, preferred_element_type=F32)
        out_ref[j] += total


def bin_own(gathered, moveout, groups, shots):
    nz = gathered.shape[0]
    tables, stencil = moveout.shape[1:]
    weights = jnp.transpose(moveout, (0, 2, 1)).reshape(2 * stencil, tables)
    out = pl.pallas_call(
        functools.partial(bin_kernel, groups, tables, shots),
        grid=(nz,),
        out_shape=jax.ShapeDtypeStruct((stencil, 2 * shots, groups), F32),
        in_specs=[
            pl.BlockSpec(weights.shape, lambda i: (0, 0)),
            pl.BlockSpec((1,) + gathered.shape[1:], lambda i: (i, 0, 0, 0)),
        ],
        out_specs=pl.BlockSpec((stencil, 2 * shots, groups), lambda i: (0, 0, 0)),
        name="bin_own",
    )(weights, gathered)
    return jnp.transpose(out, (1, 2, 0)).reshape(2, shots, groups * stencil)


def multiply_kernel(ns, shots, steps, p_ref, a_ref, out_ref, high, low, sent, got, ss, rs):
    step = pl.program_id(0)
    c = lax.axis_index("src")
    half = ns * shots
    tile = a_ref.shape[1]

    @pl.when(step == 0)
    def _():
        barrier = pltpu.get_barrier_semaphore()
        for off in range(1, ns):
            pl.semaphore_signal(
                barrier, inc=1, device_id={"src": lax.rem(c + off, ns)}, device_id_type=MESH
            )
        for part in (0, 1):
            top, rest = split(p_ref[part])
            high[part * half : (part + 1) * half, :] = top
            low[part * half : (part + 1) * half, :] = rest
        pl.semaphore_wait(barrier, ns - 1)

    def times(part):
        top, rest = split(a_ref[part])
        total = lax.dot_general(high[...], top, NT, preferred_element_type=F32)
        total += lax.dot_general(low[...], top, NT, preferred_element_type=F32)
        total += lax.dot_general(high[...], rest, NT, preferred_element_type=F32)
        return total

    by_real = times(0)
    by_imag = times(1)
    sent[step, 0] = by_real[:half] - by_imag[half:]
    sent[step, 1] = by_imag[:half] + by_real[half:]

    def copy(at, off):
        who = lax.rem(c + off, ns)
        return remote(
            sent.at[at, :, pl.ds(pl.multiple_of(who * shots, 8), shots), :],
            got.at[off - 1, at],
            ss.at[off - 1, at],
            rs.at[off - 1, at],
            {"src": who},
        )

    for off in range(1, ns):
        copy(step, off).start()

    @pl.when(step == steps - 1)
    def _():
        mine = pl.ds(pl.multiple_of(c * shots, 8), shots)
        for at in range(steps):
            for off in range(1, ns):
                copy(at, off).wait_recv()
            total = sent[at, :, mine, :]
            for off in range(1, ns):
                total += got[off - 1, at]
            out_ref[:, :, at * tile : (at + 1) * tile] = total
        for at in range(steps):
            for off in range(1, ns):
                copy(at, off).wait_send()


def multiply(columns, aperture, ns, cid):
    _, half, depth = columns.shape
    outs = aperture.shape[1]
    shots = half // ns
    tile = min(outs, 256)
    steps = outs // tile
    dma = pltpu.SemaphoreType.DMA
    return pl.pallas_call(
        functools.partial(multiply_kernel, ns, shots, steps),
        grid=(steps,),
        out_shape=jax.ShapeDtypeStruct((2, shots, outs), F32),
        in_specs=[
            pl.BlockSpec(memory_space=pltpu.VMEM),
            pl.BlockSpec((2, tile, depth), lambda i: (0, i, 0)),
        ],
        out_specs=pl.BlockSpec(memory_space=pltpu.VMEM),
        scratch_shapes=[
            pltpu.VMEM((2 * half, depth), BF16),
            pltpu.VMEM((2 * half, depth), BF16),
            pltpu.VMEM((steps, 2, half, tile), F32),
            pltpu.VMEM((ns - 1, steps, 2, shots, tile), F32),
            dma((ns - 1, steps)),
            dma((ns - 1, steps)),
        ],
        name="multiply",
        compiler_params=pltpu.CompilerParams(
            collective_id=cid,
            has_side_effects=True,
            dimension_semantics=("arbitrary",),
            vmem_limit_bytes=56 << 20,
        ),
    )(columns, aperture)


def per_device(nz, ns, traces, moveout, owner, group, table, aperture, shaping):
    groups = aperture.shape[1] // moveout.shape[2]
    shots = traces.shape[0]
    width = traces.shape[2]
    codes = jnp.stack([owner, group, table]).astype(F32)
    codes = jnp.concatenate([codes, jnp.zeros((5, width), F32)])
    flat = jnp.transpose(traces, (1, 0, 2)).reshape(2 * shots, width)
    sources = gather(jnp.concatenate([flat, codes])[None], nz, ns, False, 3, 0, "gather_traces")
    binned = bin_own(sources, moveout, groups, shots)
    form = jnp.transpose(shaping, (1, 0, 2))
    panel = binned
    for sweep in range(ITERS):
        columns = gather(panel, nz, ns, True, 4, 1, "gather_panel")
        found = multiply(columns, aperture, ns, 2)
        panel = jnp.stack(
            [
                binned[0] - (form[0] * found[0] - form[1] * found[1]),
                binned[1] - (form[0] * found[1] + form[1] * found[0]),
            ]
        )
    return jnp.transpose(panel, (1, 0, 2))


def solution(mesh):
    nz, ns = mesh.shape["rcv"], mesh.shape["src"]
    in_specs = (
        P(("freq", "src"), None, "rcv"),
        P(None, "freq", None),
        P(("freq", "rcv")),
        P(("freq", "rcv")),
        P(("freq", "rcv")),
        P(None, ("freq", "rcv"), "src"),
        P(("freq", "src"), None, "rcv"),
    )
    out_specs = P(("freq", "src"), None, "rcv")
    return jax.shard_map(
        functools.partial(per_device, nz, ns),
        mesh=mesh,
        in_specs=in_specs,
        out_specs=out_specs,
        check_vma=False,
    )
```

time: 582 us -> 204 us (0.35)
  waiting for transfers between devices: 324 us -> 0 us
  Pallas kernels: 0 us -> 189 us
  matrix products: 146 us -> 0 us
  other arithmetic: 73.9 us -> 4.65 us
  local copies, waits for them, and re-layouts: 23.4 us -> 9.64 us
  between operations: 13.6 us -> 0.15 us
    pallas_call x0 -> x6, Pallas kernels: none -> 189 us  [the longest x3 112 us: gather(): pl.pallas_call(functools.partial(gather_kernel, nz, ns, fold, plane, cuts...]
    psum x2 -> x0, waiting for transfers between devices: 172 us -> none  [from_root(): return lax.psum(kept, axis)]
    dot_general x6 -> x0, matrix products: 145 us -> none  [the longest x4 79.2 us: interpolate(): jnp.einsum('sct,tdb->scdb', values, matrix, precision=lax.Precision.HIGHEST)]
    reduce_scatter x3 -> x0, waiting for transfers between devices: 106 us -> none  [the longest x2 59.2 us: multiply(): lax.psum_scatter(complex_join(jnp.einsum('sck,dik->scdi', columns, apertu...]
    mul x8 -> x0, other arithmetic: 51.8 us -> none  [the longest x4 48.9 us: bin_matrix(): matrix = group_hot[:, None, :, None] * weights[:, :, None, :]]
    all_gather x2 -> x0, waiting for transfers between devices: 46 us -> none  [to_columns(): shots_all = lax.all_gather(panel_now, 'src', axis=0, tiled=True)]
    mul x4 -> x0, local copies, waits for them, and re-layouts: 17.3 us -> none  [bin_matrix(): matrix = group_hot[:, None, :, None] * weights[:, :, None, :]]
    select_n x2 -> x0, other arithmetic: 6.28 us -> none  [from_root(): jnp.where(lax.axis_index(axis) == source, value, 0).astype(value.dtype)]
  transfers between devices with their start and end apart: 7 -> 0, of which waited for: 7 -> 0; matrix products, arithmetic and copies ran while one was open for 0% -> 0% of each run, Pallas kernels for 0% -> 0%
where the time goes in v1:
time: 204 us; the launch traced here: 203 us
  Pallas kernels  189 us (93%)
  local copies, waits for them, and re-layouts  9.64 us (5%)
  other arithmetic  4.65 us (2%)
    pallas_call x3, Pallas kernels, gather(): pl.pallas_call(functools.partial(gather_kernel, nz, ns, fold, plane, cuts...  112 us
    pallas_call x2, Pallas kernels, multiply(): pl.pallas_call(functools.partial(multiply_kernel, ns, shots, steps), grid...  61.8 us
    pallas_call x1, Pallas kernels, bin_own(): pl.pallas_call(functools.partial(bin_kernel, groups, tables, shots), grid...  14.8 us

profile of v1, /device:TPU:0, one launch (start us, length us, event | category | flops | bytes accessed | tf_op | source)
XLA Modules:
  0.0 203.3 jit_solution(13029866760999367302)
XLA Ops:
  0.0 1.0 copy.14
  1.0 0.7 add_convert_fusion
  1.8 0.1 pad.6.clone
  1.9 0.8 maximum_bitcast_fusion.1.in_ref
  2.7 26.4 %gather_traces.1.x_ref = f32[4,1,72,1024]{3,2,1,0:T(8,128)} custom-call(f32[1,72,1024]{2,1,0:T(8,128)} %maximum_bitcast_fusion.1.in_ref), custom_call_target="tpu_custom_call" | custom-call | tf_op jit(solution)/shard_map/gather_traces/pallas_call | solution.py:201
  29.1 14.8 %bin_own.1 = f32[16,64,128]{2,1,0:T(8,128)} custom-call(f32[32,32]{1,0:T(8,128)} %bitcast.28, f32[4,1,72,1024]{3,2,1,0:T(8,128)} %gather_traces.1.x_ref), custom_call_target="tpu_custom_call" | custom-call | tf_op jit(solution)/shard_map/bin_own/pallas_call | solution.py:253
  44.0 1.1 fusion
  45.0 0.5 copy.20
  45.5 0.0 copy-start
  45.5 0.3 copy.21
  45.8 0.5 copy.15
  46.4 1.0 copy.22
  47.4 0.0 copy-done
  47.4 0.5 copy.17
  47.9 1.2 reshape.19
  49.0 2.0 copy.18.in_ref
  51.0 42.2 %gather_panel.2.p_ref = f32[2,128,2048]{2,1,0:T(8,128)} custom-call(f32[2,32,2048]{2,1,0:T(8,128)} %copy.18.in_ref), custom_call_target="tpu_custom_call" | custom-call | tf_op jit(solution)/shard_map/gather_panel/pallas_call | solution.py:201
  93.2 0.0 copy-start.2
  93.2 0.0 copy-start.1
  93.2 30.9 %multiply.2 = f32[2,32,2048]{2,1,0:T(8,128)} custom-call(f32[2,128,2048]{2,1,0:T(8,128)} %gather_panel.2.p_ref, f32[2,2048,2048]{2,1,0:T(8,128)} %a_ref.3), custom_call_target="tpu_custom_call" | custom-call | tf_op jit(solution)/shard_map/multiply/pallas_call | solution.py:333
  124.2 0.0 copy-done.2
  124.2 0.3 copy.26
  124.5 0.0 copy-done.1
  124.5 1.1 subtract_subtract_fusion.1
  125.6 0.8 pad_maximum_fusion.in_ref
  126.4 43.6 %gather_panel.3.p_ref = f32[2,128,2048]{2,1,0:T(8,128)} custom-call(f32[2,32,2048]{2,1,0:T(8,128)} %pad_maximum_fusion.in_ref), custom_call_target="tpu_custom_call" | custom-call | tf_op jit(solution)/shard_map/gather_panel/pallas_call | solution.py:201
  170.0 30.9 %multiply.3 = f32[2,32,2048]{2,1,0:T(8,128)} custom-call(f32[2,128,2048]{2,1,0:T(8,128)} %gather_panel.3.p_ref, f32[2,2048,2048]{2,1,0:T(8,128)} %a_ref.3), custom_call_target="tpu_custom_call" | custom-call | tf_op jit(solution)/shard_map/multiply/pallas_call | solution.py:333
  200.9 1.1 subtract_subtract_fusion
  202.1 1.2 copy.24
  (2 shorter events, 0.0 us)
Async XLA Ops:
  45.5 1.8 copy-start
  93.2 31.0 %copy-start.2 = (f32[32,2,2048]{2,1,0:T(2,128)S(1)}, f32[32,2,2048]{2,1,0:T(2,128)}, u32[]{:S(2)}) copy-start(f32[32,2,2048]{2,1,0:T(2,128)} %param.13) | copy-start | bytes 1572868
  93.2 31.3 %copy-start.1 = (f32[1,32,2048]{2,1,0:T(8,128)S(1)}, f32[1,32,2048]{2,1,0:T(8,128)}, u32[]{:S(2)}) copy-start(f32[1,32,2048]{2,1,0:T(8,128)} %copy.22) | copy-start | bytes 786436

commit v2 on v1

--- a/solution.py
+++ b/solution.py
@@ -209,7 +209,7 @@
     )(value)
 
 
-def bin_kernel(groups, tables, shots, wt_ref, x_ref, out_ref):
+def bin_kernel(groups, tables, shots, wt_ref, x_ref, out_ref, terms, total, order):
     stencil = wt_ref.shape[0] // 2
     rows = 2 * shots
     width = x_ref.shape[-1]
@@ -232,56 +232,103 @@
     real = x_ref[0, 0, 0:shots, :]
     imag = x_ref[0, 0, shots:rows, :]
 
-    @pl.when(pl.program_id(0) == 0)
-    def _():
-        out_ref[...] = jnp.zeros_like(out_ref)
-
     for j in range(stencil):
         wr = picked[j : j + 1, :]
         wi = picked[stencil + j : stencil + j + 1, :]
-        both = jnp.concatenate([real * wr - imag * wi, real * wi + imag * wr], axis=0)
-        high, low = split(both)
-        total = lax.dot_general(high, hot, NT, preferred_element_type=F32)
-        total += lax.dot_general(low, hot, NT, preferred_element_type=F32)
-        out_ref[j] += total
+        base = j * 2 * rows
+        for part, both in enumerate((real * wr - imag * wi, real * wi + imag * wr)):
+            high, low = split(both)
+            at = base + part * shots
+            terms[at : at + shots, :] = high
+            terms[at + rows : at + rows + shots, :] = low
+
+    found = lax.dot_general(terms[...], hot, NT, preferred_element_type=F32)
+    found = found.reshape(stencil, 2, rows, groups)
+    found = found[:, 0] + found[:, 1]
+
+    @pl.when(pl.program_id(0) == 0)
+    def _():
+        total[...] = found
+
+    @pl.when(pl.program_id(0) > 0)
+    def _():
+        total[...] += found
+
+    @pl.when(pl.program_id(0) == pl.num_programs(0) - 1)
+    def _():
+        for j in range(stencil):
+            order[:, j, :] = total[j].T
+        out_ref[...] = order[...].reshape(groups * stencil, rows).T
 
 
 def bin_own(gathered, moveout, groups, shots):
     nz = gathered.shape[0]
     tables, stencil = moveout.shape[1:]
+    width = gathered.shape[-1]
     weights = jnp.transpose(moveout, (0, 2, 1)).reshape(2 * stencil, tables)
     out = pl.pallas_call(
         functools.partial(bin_kernel, groups, tables, shots),
         grid=(nz,),
-        out_shape=jax.ShapeDtypeStruct((stencil, 2 * shots, groups), F32),
+        out_shape=jax.ShapeDtypeStruct((2 * shots, groups * stencil), F32),
         in_specs=[
             pl.BlockSpec(weights.shape, lambda i: (0, 0)),
             pl.BlockSpec((1,) + gathered.shape[1:], lambda i: (i, 0, 0, 0)),
         ],
-        out_specs=pl.BlockSpec((stencil, 2 * shots, groups), lambda i: (0, 0, 0)),
+        out_specs=pl.BlockSpec((2 * shots, groups * stencil), lambda i: (0, 0)),
+        scratch_shapes=[
+            pltpu.VMEM((stencil * 4 * shots, width), BF16),
+            pltpu.VMEM((stencil, 2 * shots, groups), F32),
+            pltpu.VMEM((groups, stencil, 2 * shots), F32),
+        ],
         name="bin_own",
     )(weights, gathered)
-    return jnp.transpose(out, (1, 2, 0)).reshape(2, shots, groups * stencil)
-
-
-def multiply_kernel(ns, shots, steps, p_ref, a_ref, out_ref, high, low, sent, got, ss, rs):
+    return out.reshape(2, shots, groups * stencil)
+
+
+def multiply_kernel(
+    ns, shots, steps, p_ref, a_ref, out_ref, high, low, mine, give, take, pass_on, got, s1, r1, s2, r2
+):
     step = pl.program_id(0)
     c = lax.axis_index("src")
+    core = lax.rem(c, 2)
+    chip = c // 2
+    chips = ns // 2
     half = ns * shots
     tile = a_ref.shape[1]
 
     @pl.when(step == 0)
     def _():
         barrier = pltpu.get_barrier_semaphore()
-        for off in range(1, ns):
-            pl.semaphore_signal(
-                barrier, inc=1, device_id={"src": lax.rem(c + off, ns)}, device_id_type=MESH
-            )
+        pl.semaphore_signal(barrier, inc=1, device_id={"src": c + 1 - 2 * core}, device_id_type=MESH)
+        for off in range(1, chips):
+            who = 2 * lax.rem(chip + off, chips) + core
+            pl.semaphore_signal(barrier, inc=1, device_id={"src": who}, device_id_type=MESH)
         for part in (0, 1):
             top, rest = split(p_ref[part])
             high[part * half : (part + 1) * half, :] = top
             low[part * half : (part + 1) * half, :] = rest
-        pl.semaphore_wait(barrier, ns - 1)
+        pl.semaphore_wait(barrier, chips)
+
+    def to_partner(at):
+        return remote(give.at[at], take.at[at], s1.at[at], r1.at[at], {"src": c + 1 - 2 * core})
+
+    def to_chip(at, off):
+        who = 2 * lax.rem(chip + off, chips) + core
+        return remote(
+            pass_on.at[at, off - 1],
+            got.at[at, off - 1],
+            s2.at[at, off - 1],
+            r2.at[at, off - 1],
+            {"src": who},
+        )
+
+    def reduce_pair(at):
+        to_partner(at).wait_recv()
+        for off in range(1, chips):
+            there = lax.rem(chip + off, chips)
+            pass_on[at, off - 1] = mine[at, there] + take[at, there]
+            to_chip(at, off).start()
+        mine[at, chip] += take[at, chip]
 
     def times(part):
         top, rest = split(a_ref[part])
@@ -292,35 +339,38 @@
 
     by_real = times(0)
     by_imag = times(1)
-    sent[step, 0] = by_real[:half] - by_imag[half:]
-    sent[step, 1] = by_imag[:half] + by_real[half:]
-
-    def copy(at, off):
-        who = lax.rem(c + off, ns)
-        return remote(
-            sent.at[at, :, pl.ds(pl.multiple_of(who * shots, 8), shots), :],
-            got.at[off - 1, at],
-            ss.at[off - 1, at],
-            rs.at[off - 1, at],
-            {"src": who},
-        )
-
-    for off in range(1, ns):
-        copy(step, off).start()
+    both = (by_real[:half] - by_imag[half:], by_imag[:half] + by_real[half:])
+    for part in (0, 1):
+        for who in range(ns):
+            value = both[part][who * shots : (who + 1) * shots]
+
+            @pl.when(core == who % 2)
+            def _():
+                mine[step, who // 2, part] = value
+
+            @pl.when(core != who % 2)
+            def _():
+                give[step, who // 2, part] = value
+
+    to_partner(step).start()
+
+    @pl.when(step > 0)
+    def _():
+        reduce_pair(step - 1)
 
     @pl.when(step == steps - 1)
     def _():
-        mine = pl.ds(pl.multiple_of(c * shots, 8), shots)
+        reduce_pair(step)
         for at in range(steps):
-            for off in range(1, ns):
-                copy(at, off).wait_recv()
-            total = sent[at, :, mine, :]
-            for off in range(1, ns):
-                total += got[off - 1, at]
+            total = mine[at, chip]
+            for off in range(1, chips):
+                to_chip(at, off).wait_recv()
+                total += got[at, off - 1]
             out_ref[:, :, at * tile : (at + 1) * tile] = total
         for at in range(steps):
-            for off in range(1, ns):
-                copy(at, off).wait_send()
+            to_partner(at).wait_send()
+            for off in range(1, chips):
+                to_chip(at, off).wait_send()
 
 
 def multiply(columns, aperture, ns, cid):
@@ -329,7 +379,9 @@
     shots = half // ns
     tile = min(outs, 256)
     steps = outs // tile
+    chips = ns // 2
     dma = pltpu.SemaphoreType.DMA
+    block = (2, shots, tile)
     return pl.pallas_call(
         functools.partial(multiply_kernel, ns, shots, steps),
         grid=(steps,),
@@ -342,10 +394,15 @@
         scratch_shapes=[
             pltpu.VMEM((2 * half, depth), BF16),
             pltpu.VMEM((2 * half, depth), BF16),
-            pltpu.VMEM((steps, 2, half, tile), F32),
-            pltpu.VMEM((ns - 1, steps, 2, shots, tile), F32),
-            dma((ns - 1, steps)),
-            dma((ns - 1, steps)),
+            pltpu.VMEM((steps, chips) + block, F32),
+            pltpu.VMEM((steps, chips) + block, F32),
+            pltpu.VMEM((steps, chips) + block, F32),
+            pltpu.VMEM((steps, chips - 1) + block, F32),
+            pltpu.VMEM((steps, chips - 1) + block, F32),
+            dma((steps,)),
+            dma((steps,)),
+            dma((steps, chips - 1)),
+            dma((steps, chips - 1)),
         ],
         name="multiply",
         compiler_params=pltpu.CompilerParams(
@@ -369,7 +426,7 @@
     form = jnp.transpose(shaping, (1, 0, 2))
     panel = binned
     for sweep in range(ITERS):
-        columns = gather(panel, nz, ns, True, 4, 1, "gather_panel")
+        columns = gather(panel, nz, ns, True, 8, 1, "gather_panel")
         found = multiply(columns, aperture, ns, 2)
         panel = jnp.stack(
             [

time: 204 us -> 182 us (0.89)
  Pallas kernels: 189 us -> 173 us
  local copies, waits for them, and re-layouts: 9.64 us -> 3.67 us
    pallas_call x2, Pallas kernels: 61.8 us -> 53.3 us  [multiply(): pl.pallas_call(functools.partial(multiply_kernel, ns, shots, steps), grid...]
    pallas_call x1, Pallas kernels: 14.8 us -> 8.77 us  [bin_own(): pl.pallas_call(functools.partial(bin_kernel, groups, tables, shots), grid...]
    reshape x2 -> x0, local copies, waits for them, and re-layouts: 3.13 us -> none  [bin_own(): return jnp.transpose(out, (1, 2, 0)).reshape(2, shots, groups * stencil)]
    sub x2 -> x0, other arithmetic: 2.24 us -> none  [per_device(): binned[0] - (form[0] * found[0] - form[1] * found[1])]
    another operation x1 -> x3, other arithmetic: 0.83 us -> 3.06 us  [per_device(): jnp.stack([binned[0] - (form[0] * found[0] - form[1] * found[1]), binned[...]
    slice x3 -> x0, local copies, waits for them, and re-layouts: 2.06 us -> none  [the longest x2 1.57 us: per_device(): binned[0] - (form[0] * found[0] - form[1] * found[1])]
where the time goes in v2:
time: 182 us; the launch traced here: 181 us
  Pallas kernels  173 us (95%)
  other arithmetic  4.63 us (3%)
  local copies, waits for them, and re-layouts  3.67 us (2%)
    pallas_call x3, Pallas kernels, gather(): pl.pallas_call(functools.partial(gather_kernel, nz, ns, fold, plane, cuts...  111 us
    pallas_call x2, Pallas kernels, multiply(): pl.pallas_call(functools.partial(multiply_kernel, ns, shots, steps), grid...  53.3 us
    pallas_call x1, Pallas kernels, bin_own(): pl.pallas_call(functools.partial(bin_kernel, groups, tables, shots), grid...  8.77 us

profile of v2, /device:TPU:0, one launch (start us, length us, event | category | flops | bytes accessed | tf_op | source)
XLA Modules:
  0.0 181.1 jit_solution(17860934141403977780)
XLA Ops:
  0.0 0.1 pad.6.clone
  0.1 0.7 add_convert_fusion
  0.8 1.0 copy.8
  1.9 0.8 maximum_bitcast_fusion.1.in_ref
  2.7 1.3 copy.12
  4.0 26.5 %gather_traces.1.x_ref = f32[4,1,72,1024]{3,2,1,0:T(8,128)} custom-call(f32[1,72,1024]{2,1,0:T(8,128)} %maximum_bitcast_fusion.1.in_ref), custom_call_target="tpu_custom_call" | custom-call | tf_op jit(solution)/shard_map/gather_traces/pallas_call | solution.py:201
  30.5 8.8 %bin_own.1 = f32[64,2048]{1,0:T(8,128)} custom-call(f32[32,32]{1,0:T(8,128)} %bitcast.45, f32[4,1,72,1024]{3,2,1,0:T(8,128)} %gather_traces.1.x_ref), custom_call_target="tpu_custom_call" | custom-call | tf_op jit(solution)/shard_map/bin_own/pallas_call | solution.py:269
  39.2 41.8 %gather_panel.2.p_ref = f32[2,128,2048]{2,1,0:T(8,128)} custom-call(f32[2,32,2048]{2,1,0:T(8,128)} %bitcast.40), custom_call_target="tpu_custom_call" | custom-call | tf_op jit(solution)/shard_map/gather_panel/pallas_call | solution.py:201
  81.1 0.0 copy-start
  81.1 26.7 %multiply.2 = f32[2,32,2048]{2,1,0:T(8,128)} custom-call(f32[2,128,2048]{2,1,0:T(8,128)} %gather_panel.2.p_ref, f32[2,2048,2048]{2,1,0:T(8,128)} %a_ref.3), custom_call_target="tpu_custom_call" | custom-call | tf_op jit(solution)/shard_map/multiply/pallas_call | solution.py:385
  107.8 0.0 copy-done
  107.8 1.1 fusion.3
  108.9 0.8 pad_maximum_fusion.in_ref
  109.7 42.4 %gather_panel.3.p_ref = f32[2,128,2048]{2,1,0:T(8,128)} custom-call(f32[2,32,2048]{2,1,0:T(8,128)} %pad_maximum_fusion.in_ref), custom_call_target="tpu_custom_call" | custom-call | tf_op jit(solution)/shard_map/gather_panel/pallas_call | solution.py:201
  152.1 26.6 %multiply.3 = f32[2,32,2048]{2,1,0:T(8,128)} custom-call(f32[2,128,2048]{2,1,0:T(8,128)} %gather_panel.3.p_ref, f32[2,2048,2048]{2,1,0:T(8,128)} %a_ref.3), custom_call_target="tpu_custom_call" | custom-call | tf_op jit(solution)/shard_map/multiply/pallas_call | solution.py:385
  178.8 1.1 fusion.1
  179.9 1.2 copy.10
  (2 shorter events, 0.0 us)
Async XLA Ops:
  81.1 26.7 %copy-start = (f32[64,2048]{1,0:T(8,128)S(1)}, f32[64,2048]{1,0:T(8,128)}, u32[]{:S(2)}) copy-start(f32[64,2048]{1,0:T(8,128)} %bin_own.1) | copy-start | bytes 1572868

commit v3 on v2

--- a/solution.py
+++ b/solution.py
@@ -209,80 +209,204 @@
     )(value)
 
 
-def bin_kernel(groups, tables, shots, wt_ref, x_ref, out_ref, terms, total, order):
+def bin_kernel(
+    nz, cuts, groups, tables, shots, in_ref, wt_ref, out_ref, held, terms, total, order, zs, zr
+):
+    z = lax.axis_index("rcv")
     stencil = wt_ref.shape[0] // 2
     rows = 2 * shots
-    width = x_ref.shape[-1]
-    me = lax.axis_index("rcv").astype(F32)
-    owner = x_ref[0, 0, rows : rows + 1, :]
-    group = x_ref[0, 0, rows + 1 : rows + 2, :]
-    table = x_ref[0, 0, rows + 2 : rows + 3, :]
-    table_ids = lax.broadcasted_iota(jnp.int32, (tables, width), 0).astype(F32)
-    table_hot = (table_ids == table).astype(BF16)
+    width = in_ref.shape[-1]
+    cells = nz * groups
+
+    def has(lane):
+        near = z + 1 - 2 * lane
+        return (near >= 0) & (near < nz)
+
+    barrier = pltpu.get_barrier_semaphore()
+    for lane in (0, 1):
+
+        @pl.when(has(lane))
+        def _():
+            pl.semaphore_signal(
+                barrier, inc=1, device_id={"rcv": z + 1 - 2 * lane}, device_id_type=MESH
+            )
+
+    pl.semaphore_wait(barrier, jnp.where(z > 0, 1, 0) + jnp.where(z < nz - 1, 1, 0))
+
+    def along(own, block, lane, dist, q):
+        cut = cuts[q]
+        return remote(
+            in_ref.at[cut] if own else held.at[(block,) + cut],
+            held.at[(block,) + cut],
+            zs.at[lane, dist, q],
+            zr.at[lane, dist, q],
+            {"rcv": z + 1 - 2 * lane},
+        )
+
+    for q in range(len(cuts)):
+        for lane in (0, 1):
+
+            @pl.when(has(lane))
+            def _():
+                along(True, z, lane, 0, q).start()
+
     w = wt_ref[...]
     w0 = w.astype(BF16)
     rest = w - w0.astype(F32)
     w1 = rest.astype(BF16)
     w2 = (rest - w1.astype(F32)).astype(BF16)
-    picked = sum(
-        jnp.dot(part, table_hot, preferred_element_type=F32) for part in (w0, w1, w2)
-    )
-    group_ids = lax.broadcasted_iota(jnp.int32, (groups, width), 0).astype(F32)
-    hot = ((group_ids == group) & (owner == me)).astype(BF16)
-    real = x_ref[0, 0, 0:shots, :]
-    imag = x_ref[0, 0, shots:rows, :]
-
+    table_ids = lax.broadcasted_iota(jnp.int32, (tables, width), 0).astype(F32)
+    cell_ids = lax.broadcasted_iota(jnp.int32, (cells, width), 0).astype(F32)
+
+    def sums(view):
+        cell = view[0, rows : rows + 1, :] * float(groups) + view[0, rows + 1 : rows + 2, :]
+        table_hot = (table_ids == view[0, rows + 2 : rows + 3, :]).astype(BF16)
+        picked = sum(
+            jnp.dot(part, table_hot, preferred_element_type=F32) for part in (w0, w1, w2)
+        )
+        hot = (cell_ids == cell).astype(BF16)
+        real = view[0, 0:shots, :]
+        imag = view[0, shots:rows, :]
+        for j in range(stencil):
+            wr = picked[j : j + 1, :]
+            wi = picked[stencil + j : stencil + j + 1, :]
+            base = j * 2 * rows
+            for part, both in enumerate((real * wr - imag * wi, real * wi + imag * wr)):
+                high, low = split(both)
+                at = base + part * shots
+                terms[at : at + shots, :] = high
+                terms[at + rows : at + rows + shots, :] = low
+        found = lax.dot_general(terms[...], hot, NT, preferred_element_type=F32)
+        found = found.reshape(stencil, 2, rows, cells)
+        return found[:, 0] + found[:, 1]
+
+    total[...] = sums(in_ref)
+
+    def hop(dist, carry):
+        for q in range(len(cuts)):
+            for lane in (0, 1):
+                block = z - dist * (1 - 2 * lane)
+
+                @pl.when((block >= 0) & (block < nz))
+                def _():
+                    along(False, block, lane, dist - 1, q).wait_recv()
+
+                    @pl.when(has(lane))
+                    def _():
+                        along(False, block, lane, dist, q).start()
+
+        def add(lane, inner):
+            block = z - dist * (1 - 2 * lane)
+
+            @pl.when((block >= 0) & (block < nz))
+            def _():
+                total[...] += sums(held.at[block])
+
+            return inner
+
+        return lax.fori_loop(0, 2, add, carry)
+
+    lax.fori_loop(1, nz, hop, 0)
     for j in range(stencil):
-        wr = picked[j : j + 1, :]
-        wi = picked[stencil + j : stencil + j + 1, :]
-        base = j * 2 * rows
-        for part, both in enumerate((real * wr - imag * wi, real * wi + imag * wr)):
-            high, low = split(both)
-            at = base + part * shots
-            terms[at : at + shots, :] = high
-            terms[at + rows : at + rows + shots, :] = low
-
-    found = lax.dot_general(terms[...], hot, NT, preferred_element_type=F32)
-    found = found.reshape(stencil, 2, rows, groups)
-    found = found[:, 0] + found[:, 1]
-
-    @pl.when(pl.program_id(0) == 0)
-    def _():
-        total[...] = found
-
-    @pl.when(pl.program_id(0) > 0)
-    def _():
-        total[...] += found
-
-    @pl.when(pl.program_id(0) == pl.num_programs(0) - 1)
-    def _():
-        for j in range(stencil):
-            order[:, j, :] = total[j].T
-        out_ref[...] = order[...].reshape(groups * stencil, rows).T
-
-
-def bin_own(gathered, moveout, groups, shots):
-    nz = gathered.shape[0]
+        order[:, j, :] = total[j].T
+    out_ref[...] = order[...].reshape(cells * stencil, rows).T
+
+    def drain(dist, carry):
+        for q in range(len(cuts)):
+            for lane in (0, 1):
+                block = z - dist * (1 - 2 * lane)
+
+                @pl.when((block >= 0) & (block < nz) & has(lane))
+                def _():
+                    along(False, block, lane, dist, q).wait_send()
+
+        return carry
+
+    lax.fori_loop(0, nz, drain, 0)
+
+
+def bin_all(value, moveout, nz, groups, shots, cid):
     tables, stencil = moveout.shape[1:]
-    width = gathered.shape[-1]
+    width = value.shape[-1]
     weights = jnp.transpose(moveout, (0, 2, 1)).reshape(2 * stencil, tables)
+    cuts = pieces(value.shape, 3)
+    dma = pltpu.SemaphoreType.DMA
+    vmem = pl.BlockSpec(memory_space=pltpu.VMEM)
     out = pl.pallas_call(
-        functools.partial(bin_kernel, groups, tables, shots),
-        grid=(nz,),
-        out_shape=jax.ShapeDtypeStruct((2 * shots, groups * stencil), F32),
-        in_specs=[
-            pl.BlockSpec(weights.shape, lambda i: (0, 0)),
-            pl.BlockSpec((1,) + gathered.shape[1:], lambda i: (i, 0, 0, 0)),
+        functools.partial(bin_kernel, nz, cuts, groups, tables, shots),
+        out_shape=jax.ShapeDtypeStruct((2 * shots, nz * groups * stencil), F32),
+        in_specs=[vmem, vmem],
+        out_specs=vmem,
+        scratch_shapes=[
+            pltpu.VMEM((nz,) + value.shape, F32),
+            pltpu.VMEM((stencil * 4 * shots, width), BF16),
+            pltpu.VMEM((stencil, 2 * shots, nz * groups), F32),
+            pltpu.VMEM((nz * groups, stencil, 2 * shots), F32),
+            dma((2, nz, len(cuts))),
+            dma((2, nz, len(cuts))),
         ],
-        out_specs=pl.BlockSpec((2 * shots, groups * stencil), lambda i: (0, 0)),
-        scratch_shapes=[
-            pltpu.VMEM((stencil * 4 * shots, width), BF16),
-            pltpu.VMEM((stencil, 2 * shots, groups), F32),
-            pltpu.VMEM((groups, stencil, 2 * shots), F32),
-        ],
-        name="bin_own",
-    )(weights, gathered)
-    return out.reshape(2, shots, groups * stencil)
+        name="bin_all",
+        compiler_params=pltpu.CompilerParams(
+            collective_id=cid, has_side_effects=True, vmem_limit_bytes=56 << 20
+        ),
+    )(value, weights)
+    return out.reshape(2, shots, nz * groups * stencil)
+
+
+def spread_kernel(ns, in_ref, out_ref, ss, rs, ls):
+    c = lax.axis_index("src")
+    rows = in_ref.shape[1]
+    width = out_ref.shape[2]
+    barrier = pltpu.get_barrier_semaphore()
+    for off in range(1, ns):
+        pl.semaphore_signal(
+            barrier, inc=1, device_id={"src": lax.rem(c + off, ns)}, device_id_type=MESH
+        )
+    pl.semaphore_wait(barrier, ns - 1)
+
+    def part(who, p):
+        return in_ref.at[p, :, pl.ds(pl.multiple_of(who * width, 128), width)]
+
+    def place(who, p):
+        return out_ref.at[p, pl.ds(pl.multiple_of(who * rows, 8), rows), :]
+
+    sends = []
+    for off in range(1, ns):
+        for p in (0, 1):
+            who = lax.rem(c + off, ns)
+            copy = remote(
+                part(who, p), place(c, p), ss.at[off - 1, p], rs.at[off - 1, p], {"src": who}
+            )
+            copy.start()
+            sends.append(copy)
+    own = [pltpu.make_async_copy(part(c, p), place(c, p), ls.at[p]) for p in (0, 1)]
+    for copy in own:
+        copy.start()
+    for copy in own:
+        copy.wait()
+    for off in range(1, ns):
+        for p in (0, 1):
+            who = lax.rem(c + ns - off, ns)
+            remote(
+                place(who, p), place(who, p), ss.at[off - 1, p], rs.at[off - 1, p], {"src": who}
+            ).wait_recv()
+    for copy in sends:
+        copy.wait_send()
+
+
+def spread(value, ns, cid):
+    _, rows, width = value.shape
+    dma = pltpu.SemaphoreType.DMA
+    vmem = pl.BlockSpec(memory_space=pltpu.VMEM)
+    return pl.pallas_call(
+        functools.partial(spread_kernel, ns),
+        out_shape=jax.ShapeDtypeStruct((2, ns * rows, width // ns), F32),
+        in_specs=[vmem],
+        out_specs=vmem,
+        scratch_shapes=[dma((ns - 1, 2)), dma((ns - 1, 2)), dma((2,))],
+        name="spread",
+        compiler_params=pltpu.CompilerParams(collective_id=cid, has_side_effects=True),
+    )(value)
 
 
 def multiply_kernel(
@@ -421,12 +545,16 @@
     codes = jnp.stack([owner, group, table]).astype(F32)
     codes = jnp.concatenate([codes, jnp.zeros((5, width), F32)])
     flat = jnp.transpose(traces, (1, 0, 2)).reshape(2 * shots, width)
-    sources = gather(jnp.concatenate([flat, codes])[None], nz, ns, False, 3, 0, "gather_traces")
-    binned = bin_own(sources, moveout, groups, shots)
+    everyone = bin_all(jnp.concatenate([flat, codes])[None], moveout, nz, groups, shots, 0)
+    bins = aperture.shape[1]
+    binned = lax.dynamic_slice_in_dim(everyone, lax.axis_index("rcv") * bins, bins, 2)
     form = jnp.transpose(shaping, (1, 0, 2))
     panel = binned
     for sweep in range(ITERS):
-        columns = gather(panel, nz, ns, True, 8, 1, "gather_panel")
+        if sweep == 0:
+            columns = spread(everyone, ns, 3)
+        else:
+            columns = gather(panel, nz, ns, True, 8, 1, "gather_panel")
         found = multiply(columns, aperture, ns, 2)
         panel = jnp.stack(
             [

time: 182 us -> 165 us (0.907)
  Pallas kernels: 173 us -> 156 us
    pallas_call x3 -> x1, Pallas kernels: 111 us -> 42.4 us  [gather(): pl.pallas_call(functools.partial(gather_kernel, nz, ns, fold, plane, cuts...]
    pallas_call x1 -> x2, Pallas kernels: 8.77 us -> 60.6 us  [the longest x1 33.1 us: bin_all(): pl.pallas_call(functools.partial(bin_kernel, nz, cuts, groups, tables, sh...]
    sub x0 -> x2, other arithmetic: none -> 2.24 us  [per_device(): binned[0] - (form[0] * found[0] - form[1] * found[1])]
    another operation x3 -> x1, other arithmetic: 3.06 us -> 0.83 us  [per_device(): jnp.stack([binned[0] - (form[0] * found[0] - form[1] * found[1]), binned[...]
where the time goes in v3:
time: 165 us
  Pallas kernels  156 us (95%)
  other arithmetic  4.64 us (3%)
  local copies, waits for them, and re-layouts  3.67 us (2%)
    pallas_call x2, Pallas kernels, multiply(): pl.pallas_call(functools.partial(multiply_kernel, ns, shots, steps), grid...  53.4 us
    pallas_call x1, Pallas kernels, gather(): pl.pallas_call(functools.partial(gather_kernel, nz, ns, fold, plane, cuts...  42.4 us
    pallas_call x1, Pallas kernels, bin_all(): pl.pallas_call(functools.partial(bin_kernel, nz, cuts, groups, tables, sh...  33.1 us
    pallas_call x1, Pallas kernels, spread(): pl.pallas_call(functools.partial(spread_kernel, ns), out_shape=jax.ShapeD...  27.5 us

profile of v3, /device:TPU:0, one launch (start us, length us, event | category | flops | bytes accessed | tf_op | source)
XLA Modules:
  0.0 164.8 jit_solution(3329640570147301910)
XLA Ops:
  0.0 0.1 pad.6.clone
  0.1 0.7 add_convert_fusion
  0.8 1.0 copy.8
  1.9 0.8 maximum_bitcast_fusion.1.in_ref
  2.7 1.3 copy.12
  4.0 33.1 %bin_all.1 = f32[64,8192]{1,0:T(8,128)} custom-call(f32[1,72,1024]{2,1,0:T(8,128)} %maximum_bitcast_fusion.1.in_ref, f32[32,32]{1,0:T(8,128)} %bitcast.23), custom_call_target="tpu_custom_call" | custom-call | tf_op jit(solution)/shard_map/bin_all/pallas_call | solution.py:335
  37.1 27.5 %spread.1.p_ref = f32[2,128,2048]{2,1,0:T(8,128)} custom-call(f32[2,32,8192]{2,1,0:T(8,128)} %bitcast.16), custom_call_target="tpu_custom_call" | custom-call | tf_op jit(solution)/shard_map/spread/pallas_call | solution.py:401
  64.6 0.0 copy-start
  64.6 26.8 %multiply.2 = f32[2,32,2048]{2,1,0:T(8,128)} custom-call(f32[2,128,2048]{2,1,0:T(8,128)} %spread.1.p_ref, f32[2,2048,2048]{2,1,0:T(8,128)} %a_ref.3), custom_call_target="tpu_custom_call" | custom-call | tf_op jit(solution)/shard_map/multiply/pallas_call | solution.py:509
  91.4 0.0 copy-done
  91.4 1.1 subtract_subtract_fusion.1
  92.5 0.8 pad_maximum_fusion.in_ref
  93.4 42.4 %gather_panel.1.p_ref = f32[2,128,2048]{2,1,0:T(8,128)} custom-call(f32[2,32,2048]{2,1,0:T(8,128)} %pad_maximum_fusion.in_ref), custom_call_target="tpu_custom_call" | custom-call | tf_op jit(solution)/shard_map/gather_panel/pallas_call | solution.py:201
  135.8 26.6 %multiply.3 = f32[2,32,2048]{2,1,0:T(8,128)} custom-call(f32[2,128,2048]{2,1,0:T(8,128)} %gather_panel.1.p_ref, f32[2,2048,2048]{2,1,0:T(8,128)} %a_ref.3), custom_call_target="tpu_custom_call" | custom-call | tf_op jit(solution)/shard_map/multiply/pallas_call | solution.py:509
  162.4 1.1 subtract_subtract_fusion
  163.6 1.2 copy.10
  (2 shorter events, 0.0 us)
Async XLA Ops:
  64.6 26.8 %copy-start = (f32[64,8192]{1,0:T(8,128)S(1)}, f32[64,8192]{1,0:T(8,128)}, u32[]{:S(2)}) copy-start(f32[64,8192]{1,0:T(8,128)} %bin_all.1) | copy-start | bytes 6291460
